TPU v7x, 32 devices: a whole 2x2x4 slice. The times are simulated.
32 devices in a mesh: dom: 2 (over x), tok: 16 (over z, y, core).
Axes of the slice: x: 2, y: 2, z: 4, core: 2. Of those that a mesh axis runs over, the one named last changes fastest.
Arguments:
- tokens: bfloat16 [512, 4096], P(('dom', 'tok')), parts along dimension 0, may hold values from -6 to 6
- rotation_flip: int32 [4096], replicated, may hold values from 0 to 1
- gate_up: bfloat16 [4, 4096, 16384], P('dom', None, 'tok'), parts along dimension 0, may hold values from -0.09375 to 0.09375
- quant_codes: bfloat16 [4, 4096, 16384], P('dom', None, 'tok'), parts along dimension 0, may hold values from -7 to 7
- quant_exps: int32 [4, 32, 16384], P('dom', None, 'tok'), parts along dimension 0, may hold values from -10 to -7
- down_rows: bfloat16 [32768, 4096], P(('dom', 'tok')), parts along dimension 0, may hold values from -0.046875 to 0.046875
Outputs:
- correction: bfloat16 [32768, 4096], P(('dom', 'tok')), parts along dimension 0
There are 2 independent parts, one for each index of `dom`. A program takes and returns all parts, laid end to end along the dimension named above; an argument that names none is the same for every part. Nothing has to cross between parts.
All inputs are finite; a program needn't handle non-finite values.
Results may differ from a plain program's by a relative error of at most 0.012.
Values may be sent and summed in bfloat16 or wider, within the bound.
No kernel may reach another device: no remote copies, remote signals or barrier semaphores. Data moves between devices by JAX's collectives and lax.ppermute only.
A program may use at most 128 MiB of HBM per device.

v0:
```python
import jax
import jax.numpy as jnp
from jax import lax
from jax.sharding import PartitionSpec as P


def hadamard_table(order):
    index = jnp.arange(order, dtype=jnp.int32)
    common = index[:, None] & index[None, :]
    parity = jnp.zeros((order, order), jnp.int32)
    for bit_pos in range(max(order.bit_length() - 1, 1)):
        parity = parity ^ common >> bit_pos & 1
    return (1 - 2 * parity).astype(jnp.float32)


def rotate(inputs, flip):
    width = inputs.shape[-1]
    signed = inputs.astype(jnp.float32) * (1 - 2 * flip).astype(jnp.float32)
    power = width.bit_length() - 1
    outer_len = 2 ** (power // 2)
    inner_len = width // outer_len
    blocks = signed.reshape(-1, outer_len, inner_len)
    mixed = jnp.einsum(
        "ab,nbc,cd->nad",
        hadamard_table(outer_len),
        blocks,
        hadamard_table(inner_len),
        precision=lax.Precision.HIGHEST,
    )
    return (mixed.reshape(-1, width) * (1.0 / width**0.5)).astype(jnp.bfloat16)


def dequant(codes, exps):
    groups = exps.shape[1]
    scales = jnp.exp2(exps.astype(jnp.float32))
    shaped = codes.astype(jnp.float32).reshape(2, groups, codes.shape[1] // groups, codes.shape[2])
    return (shaped * scales[:, :, None, :]).reshape(codes.shape).astype(jnp.bfloat16)


def swiglu(inputs, weights):
    gate = jnp.dot(inputs, weights[0], preferred_element_type=jnp.float32)
    upper = jnp.dot(inputs, weights[1], preferred_element_type=jnp.float32)
    return (jax.nn.silu(gate) * upper).astype(jnp.bfloat16)


def per_device(tokens, rotation_flip, gate_up, quant_codes, quant_exps, down_rows):
    quant_weight = dequant(quant_codes, quant_exps)
    piece = lax.all_gather(tokens, "tok", axis=0, tiled=True)
    hid_full = swiglu(piece, gate_up)
    hid_quant = swiglu(rotate(piece, rotation_flip), quant_weight)
    mismatch = (hid_full.astype(jnp.float32) - hid_quant.astype(jnp.float32)).astype(jnp.bfloat16)
    total_tokens = mismatch.shape[0]
    partial_proj = jnp.dot(mismatch, down_rows, preferred_element_type=jnp.float32)
    projected = lax.psum(partial_proj, "tok").astype(jnp.bfloat16)
    gram = lax.dot_general(
        hid_quant, projected, (((0,), (0,)), ((), ())), preferred_element_type=jnp.float32
    )
    return (gram * (1.0 / total_tokens**0.5)).astype(jnp.bfloat16)


def solution(mesh):
    placed = (
        P(("dom", "tok"), None),
        P(),
        P("dom", None, "tok"),
        P("dom", None, "tok"),
        P("dom", None, "tok"),
        P(("dom", "tok"), None),
    )
    return jax.shard_map(
        per_device, mesh=mesh, in_specs=placed, out_specs=P(("dom", "tok"), None), check_vma=False
    )
```

profile of v0, /device:TPU:1, one launch (start us, length us, event | category | flops | bytes accessed | tf_op | source)
XLA Modules:
  0.0 203.8 jit_solution(15538142856855820026)
XLA Ops:
  6.5 0.0 all-gather.2.cloned.1.call-start
  6.5 0.7 all-gather.2.cloned.1.call-update
  7.3 1.0 multiply_exponential_fusion
  8.3 0.0 copy-start.2
  8.3 14.8 %fusion = bf16[2,4096,1024]{2,1,0:T(8,128)(2,1)} fusion(bf16[2,4096,1024]{2,1,0:T(8,128)(2,1)} %param.9, f32[2,32,1024]{2,1,0:T(8,128)S(1)} %multiply_exponential_fusion), kind=kLoop, calls=%fused_computation.1 | loop fusion | flops 25165824 | bytes 33816576 | tf_op jit(solution)/shard_map/convert_element_type | solution.py:37
  23.1 0.0 copy-done.2
  23.1 30.4 %all-gather.2.cloned.1.call-done = bf16[256,4096]{1,0:T(8,128)(2,1)} async-done(((bf16[16,4096]{1,0:T(8,128)(2,1)}), bf16[256,4096]{1,0:T(8,128)(2,1)}) %all-gather.2.cloned.1.call-update) | async-done | bytes 2097168 | tf_op jit(solution)/shard_map/all_gather | solution.py:48
  53.4 3.3 %copy.8 = bf16[256,4096]{0,1:T(8,128)(2,1)S(1)} copy(bf16[256,4096]{1,0:T(8,128)(2,1)} %all-gather.2.cloned.1.call-done) | data formatting | bytes 4194304 | tf_op jit(solution)/shard_map/all_gather | solution.py:48
  56.7 0.0 copy-start
  56.7 0.7 convert_multiply_fusion
  57.5 6.8 %fusion.11 = f32[256,64,64]{0,2,1:T(8,128)S(1)} fusion(f32[256,64,64]{0,2,1:T(8,128)S(1)} %bitcast.47), kind=kOutput, calls=%fused_computation.15 | convolution fusion | flops 805392384 | bytes 8388608 | tf_op jit(solution)/shard_map/ab,nbc,cd->nad/dot_general | solution.py:23
  64.2 6.0 %multiply_convert_fusion.1 = bf16[256,64,64]{0,2,1:T(8,128)(2,1)S(1)} fusion(f32[256,64,64]{0,2,1:T(8,128)S(1)} %fusion.11), kind=kOutput, calls=%fused_computation.17 | convolution fusion | flops 807489536 | bytes 6291456 | tf_op jit(solution)/shard_map/ab,nbc,cd->nad/dot_general | solution.py:23
  70.3 0.0 copy-done
  70.3 2.4 %fusion.2 = f32[256,1024]{1,0:T(8,128)S(1)} fusion(bf16[256,4096]{0,1:T(8,128)(2,1)S(1)} %bitcast.48, bf16[2,4096,1024]{2,1,0:T(8,128)(2,1)S(1)} %copy-done), kind=kOutput, calls=%fused_computation.6 | convolution fusion | flops 2147483648 | bytes 11534336 | tf_op jit(solution)/shard_map/dot_general | solution.py:41
  72.6 0.0 copy-start.1
  72.6 2.4 %fusion.20 = bf16[256,1024]{1,0:T(8,128)(2,1)S(1)} fusion(bf16[256,4096]{0,1:T(8,128)(2,1)S(1)} %bitcast.49, bf16[2,4096,1024]{2,1,0:T(8,128)(2,1)S(1)} %copy-done, f32[256,1024]{1,0:T(8,128)S(1)} %fusion.2), kind=kOutput, calls=%fused_computation.22 | convolution fusion | flops 2149056512 | bytes 12058624 | tf_op jit(solution)/shard_map/dot_general | solution.py:42
  75.1 0.0 copy-done.1
  75.1 6.7 %fusion.5 = f32[256,1024]{1,0:T(8,128)} fusion(bf16[256,4096]{1,0:T(8,128)(2,1)S(1)} %copy-done.1, bf16[2,4096,1024]{2,1,0:T(8,128)(2,1)} %param.8), kind=kOutput, calls=%fused_computation.9 | convolution fusion | flops 2147483648 | bytes 11534336 | tf_op jit(solution)/shard_map/dot_general | solution.py:41
  81.8 12.7 %fusion.34 = f32[256,4096]{1,0:T(8,128)} fusion(bf16[1024,4096]{1,0:T(8,128)(2,1)} %param.11, bf16[256,4096]{1,0:T(8,128)(2,1)S(1)} %copy-done.1, bf16[2,4096,1024]{2,1,0:T(8,128)(2,1)} %param.8, bf16[256,1024]{1,0:T(8,128)(2,1)S(1)} %fusion.20, f32[256,1024]{1,0:T(8,128)} %fusion.5), kind=kOutput, calls=%fused_computation.27 | convolution fusion | flops 4297588736 | bytes 24641536 | tf_op jit(solution)/shard_map/dot_general | solution.py:53
  94.5 96.6 %all-reduce.1 = bf16[256,4096]{1,0:T(8,128)(2,1)S(1)} all-reduce(f32[256,4096]{1,0:T(8,128)} %fusion.34), channel_id=1, replica_groups=mesh['dom'=2,'tok'=16] {'tok'}, use_global_device_ids=true, to_apply=%region_0.1 | all-reduce | flops 1048576 | bytes 6291456 | tf_op jit(solution)/shard_map/psum | solution.py:54
  191.1 5.8 %multiply_convert_fusion = bf16[1024,4096]{1,0:T(8,128)(2,1)} fusion(bf16[256,1024]{1,0:T(8,128)(2,1)S(1)} %fusion.20, bf16[256,4096]{1,0:T(8,128)(2,1)S(1)} %all-reduce.1), kind=kOutput, calls=%fused_computation.2 | convolution fusion | flops 2155872256 | bytes 11010048 | tf_op jit(solution)/shard_map/dot_general | solution.py:55
  (1 shorter events, 0.0 us)
Async XLA Ops:
  6.5 46.9 %all-gather.2.cloned.1.call-start = ((), (), s32[]{:S(2)}) async-start(), calls=%async_computation | async-start | bytes 2228224 | tf_op jit(solution)/shard_map/all_gather | solution.py:48
  8.3 14.8 %copy-start.2 = (s32[4096]{0:T(1024)S(1)}, s32[4096]{0:T(1024)}, u32[]{:S(2)}) copy-start(s32[4096]{0:T(1024)} %param.7) | copy-start | bytes 49156
  56.7 13.6 %copy-start = (bf16[2,4096,1024]{2,1,0:T(8,128)(2,1)S(1)}, bf16[2,4096,1024]{2,1,0:T(8,128)(2,1)}, u32[]{:S(2)}) copy-start(bf16[2,4096,1024]{2,1,0:T(8,128)(2,1)} %fusion) | copy-start | bytes 50331652
  72.6 2.5 %copy-start.1 = (bf16[256,4096]{1,0:T(8,128)(2,1)S(1)}, bf16[256,4096]{1,0:T(8,128)(2,1)}, u32[]{:S(2)}) copy-start(bf16[256,4096]{1,0:T(8,128)(2,1)} %all-gather.2.cloned.1.call-done) | copy-start | bytes 6291460
Sparse Core Ops, SparseCore 0:
  9.5 43.9 all-gather.1
where the time goes:
time: 204 us
  blocking collectives  96.6 us (47%)
  matrix products  42.8 us (21%)
  waiting for transfers between devices  31.1 us (15%)
  other arithmetic  16.5 us (8%)
  between operations  13.5 us (7%)
  local copies, waits for them, and re-layouts  3.28 us (2%)
    psum x1, blocking collectives, per_device(): projected = lax.psum(partial_proj, 'tok').astype(jnp.bfloat16)  96.6 us
    all_gather x1, waiting for transfers between devices, per_device(): piece = lax.all_gather(tokens, 'tok', axis=0, tiled=True)  30.4 us
    convert_element_type x1, other arithmetic, dequant(): (shaped * scales[:, :, None, :]).reshape(codes.shape).astype(jnp.bfloat16)  14.8 us
    dot_general x2, matrix products, rotate(): jnp.einsum('ab,nbc,cd->nad', hadamard_table(outer_len), blocks, hadamard_...  12.8 us
    dot_general x1, matrix products, per_device(): jnp.dot(mismatch, down_rows, preferred_element_type=jnp.float32)  12.7 us
    dot_general x2, matrix products, swiglu(): gate = jnp.dot(inputs, weights[0], preferred_element_type=jnp.float32)  9.03 us
    dot_general x1, matrix products, per_device(): lax.dot_general(hid_quant, projected, (((0,), (0,)), ((), ())), preferred...  5.79 us
  transfers between devices with their start and end apart: 1, of which 1 were waited for; matrix products, arithmetic and copies ran while one was open for 8% of the time, Pallas kernels for 0%

commit v1 on v0

--- a/solution.py
+++ b/solution.py
@@ -45,7 +45,12 @@
 
 def per_device(tokens, rotation_flip, gate_up, quant_codes, quant_exps, down_rows):
     quant_weight = dequant(quant_codes, quant_exps)
-    piece = lax.all_gather(tokens, "tok", axis=0, tiled=True)
+    ring = [tokens]
+    for hop in range(15):
+        ring.append(lax.ppermute(ring[-1], "tok", [(dev, (dev + 1) % 16) for dev in range(16)]))
+    piece = jnp.roll(
+        jnp.concatenate(ring[::-1], axis=0), (lax.axis_index("tok") + 1) * ring[0].shape[0], axis=0
+    )
     hid_full = swiglu(piece, gate_up)
     hid_quant = swiglu(rotate(piece, rotation_flip), quant_weight)
     mismatch = (hid_full.astype(jnp.float32) - hid_quant.astype(jnp.float32)).astype(jnp.bfloat16)

time: 204 us -> 315 us (1.54); the launches traced: 204 us -> 311 us
  local copies, waits for them, and re-layouts: 3.28 us -> 57.7 us
  waiting for transfers between devices: 31.1 us -> 78.3 us
  between operations: 13.5 us -> 0.31 us
  starting transfers between devices: 0.01 us -> 7.47 us
  blocking collectives: 96.6 us -> 102 us
  matrix products: 42.8 us -> 46.3 us
    ppermute x0 -> x15, waiting for transfers between devices: none -> 78.3 us  [per_device(): lax.ppermute(ring[-1], 'tok', [(dev, (dev + 1) % 16) for dev in range(16)])]
    concatenate x0 -> x1, local copies, waits for them, and re-layouts: none -> 32.3 us  [per_device(): jnp.roll(jnp.concatenate(ring[::-1], axis=0), (lax.axis_index('tok') + 1)...]
    all_gather x1 -> x0, waiting for transfers between devices: 30.4 us -> none  [per_device(): piece = lax.all_gather(tokens, 'tok', axis=0, tiled=True)]
    ppermute x0 -> x15, local copies, waits for them, and re-layouts: none -> 23.9 us  [per_device(): lax.ppermute(ring[-1], 'tok', [(dev, (dev + 1) % 16) for dev in range(16)])]
    ppermute x0 -> x15, starting transfers between devices: none -> 7.47 us  [per_device(): lax.ppermute(ring[-1], 'tok', [(dev, (dev + 1) % 16) for dev in range(16)])]
    dot_general x1 -> x2, matrix products: 2.44 us -> 8.32 us  [swiglu(): upper = jnp.dot(inputs, weights[1], preferred_element_type=jnp.float32)]
    psum x1, blocking collectives: 96.6 us -> 102 us  [per_device(): projected = lax.psum(partial_proj, 'tok').astype(jnp.bfloat16)]
    all_gather x1 -> x0, local copies, waits for them, and re-layouts: 3.27 us -> none  [per_device(): piece = lax.all_gather(tokens, 'tok', axis=0, tiled=True)]
  transfers between devices with their start and end apart: 1 -> 15, of which waited for: 1 -> 13; matrix products, arithmetic and copies ran while one was open for 8% -> 13% of each run, Pallas kernels for 0% -> 0%
where the time goes in v1:
time: 315 us; the launch traced here: 311 us
  blocking collectives  102 us (32%)
  waiting for transfers between devices  78.3 us (25%)
  local copies, waits for them, and re-layouts  57.7 us (18%)
  matrix products  46.3 us (15%)
  other arithmetic  18.5 us (6%)
  starting transfers between devices  7.47 us (2%)
    psum x1, blocking collectives, per_device(): projected = lax.psum(partial_proj, 'tok').astype(jnp.bfloat16)  102 us
    ppermute x15, waiting for transfers between devices, per_device(): lax.ppermute(ring[-1], 'tok', [(dev, (dev + 1) % 16) for dev in range(16)])  78.3 us
    concatenate x1, local copies, waits for them, and re-layouts, per_device(): jnp.roll(jnp.concatenate(ring[::-1], axis=0), (lax.axis_index('tok') + 1)...  32.3 us
    ppermute x15, local copies, waits for them, and re-layouts, per_device(): lax.ppermute(ring[-1], 'tok', [(dev, (dev + 1) % 16) for dev in range(16)])  23.9 us
    convert_element_type x1, other arithmetic, dequant(): (shaped * scales[:, :, None, :]).reshape(codes.shape).astype(jnp.bfloat16)  14.8 us
    dot_general x1, matrix products, per_device(): jnp.dot(mismatch, down_rows, preferred_element_type=jnp.float32)  13.5 us
    dot_general x2, matrix products, rotate(): jnp.einsum('ab,nbc,cd->nad', hadamard_table(outer_len), blocks, hadamard_...  12.8 us
    dot_general x2, matrix products, swiglu(): upper = jnp.dot(inputs, weights[1], preferred_element_type=jnp.float32)  8.32 us
  transfers between devices with their start and end apart: 15, of which 13 were waited for; matrix products, arithmetic and copies ran while one was open for 13% of the time, Pallas kernels for 0%

profile of v1, /device:TPU:1, one launch (start us, length us, event | category | flops | bytes accessed | tf_op | source)
XLA Modules:
  0.0 310.8 jit_solution(4147636821163713226)
XLA Ops:
  0.0 2.6 collective-permute-start
  9.2 2.4 collective-permute-start.2
  11.6 4.7 %collective-permute-done.2 = bf16[16,4096]{1,0:T(8,128)(2,1)S(1)} collective-permute-done((bf16[16,4096]{1,0:T(8,128)(2,1)S(1)}, bf16[16,4096]{1,0:T(8,128)(2,1)S(1)}, u32[]{:S(2)}, u32[]{:S(2)}) %collective-permute-start.2) | collective-permute-done | bytes 131104 | tf_op jit(solution)/shard_map/ppermute | solution.py:50
  16.3 7.1 %collective-permute-done.3 = bf16[16,4096]{1,0:T(8,128)(2,1)S(1)} collective-permute-done((bf16[16,4096]{1,0:T(8,128)(2,1)S(1)}, bf16[16,4096]{1,0:T(8,128)(2,1)S(1)}, u32[]{:S(2)}, u32[]{:S(2)}) %collective-permute-start.3) | collective-permute-done | bytes 131104 | tf_op jit(solution)/shard_map/ppermute | solution.py:50
  23.4 7.1 %collective-permute-done.4 = bf16[16,4096]{1,0:T(8,128)(2,1)S(1)} collective-permute-done((bf16[16,4096]{1,0:T(8,128)(2,1)S(1)}, bf16[16,4096]{1,0:T(8,128)(2,1)S(1)}, u32[]{:S(2)}, u32[]{:S(2)}) %collective-permute-start.4) | collective-permute-done | bytes 131104 | tf_op jit(solution)/shard_map/ppermute | solution.py:50
  30.5 7.1 %collective-permute-done.5 = bf16[16,4096]{1,0:T(8,128)(2,1)S(1)} collective-permute-done((bf16[16,4096]{1,0:T(8,128)(2,1)S(1)}, bf16[16,4096]{1,0:T(8,128)(2,1)S(1)}, u32[]{:S(2)}, u32[]{:S(2)}) %collective-permute-start.5) | collective-permute-done | bytes 131104 | tf_op jit(solution)/shard_map/ppermute | solution.py:50
  37.6 7.1 %collective-permute-done.6 = bf16[16,4096]{1,0:T(8,128)(2,1)S(1)} collective-permute-done((bf16[16,4096]{1,0:T(8,128)(2,1)S(1)}, bf16[16,4096]{1,0:T(8,128)(2,1)S(1)}, u32[]{:S(2)}, u32[]{:S(2)}) %collective-permute-start.6) | collective-permute-done | bytes 131104 | tf_op jit(solution)/shard_map/ppermute | solution.py:50
  44.7 7.1 %collective-permute-done.7 = bf16[16,4096]{1,0:T(8,128)(2,1)S(1)} collective-permute-done((bf16[16,4096]{1,0:T(8,128)(2,1)S(1)}, bf16[16,4096]{1,0:T(8,128)(2,1)S(1)}, u32[]{:S(2)}, u32[]{:S(2)}) %collective-permute-start.7) | collective-permute-done | bytes 131104 | tf_op jit(solution)/shard_map/ppermute | solution.py:50
  51.7 7.1 %collective-permute-done.8 = bf16[16,4096]{1,0:T(8,128)(2,1)S(1)} collective-permute-done((bf16[16,4096]{1,0:T(8,128)(2,1)S(1)}, bf16[16,4096]{1,0:T(8,128)(2,1)S(1)}, u32[]{:S(2)}, u32[]{:S(2)}) %collective-permute-start.8) | collective-permute-done | bytes 131104 | tf_op jit(solution)/shard_map/ppermute | solution.py:50
  58.8 7.1 %collective-permute-done.9 = bf16[16,4096]{1,0:T(8,128)(2,1)S(1)} collective-permute-done((bf16[16,4096]{1,0:T(8,128)(2,1)S(1)}, bf16[16,4096]{1,0:T(8,128)(2,1)S(1)}, u32[]{:S(2)}, u32[]{:S(2)}) %collective-permute-start.9) | collective-permute-done | bytes 131104 | tf_op jit(solution)/shard_map/ppermute | solution.py:50
  65.9 7.1 %collective-permute-done.10 = bf16[16,4096]{1,0:T(8,128)(2,1)S(1)} collective-permute-done((bf16[16,4096]{1,0:T(8,128)(2,1)S(1)}, bf16[16,4096]{1,0:T(8,128)(2,1)S(1)}, u32[]{:S(2)}, u32[]{:S(2)}) %collective-permute-start.10) | collective-permute-done | bytes 131104 | tf_op jit(solution)/shard_map/ppermute | solution.py:50
  73.0 7.1 %collective-permute-done.11 = bf16[16,4096]{1,0:T(8,128)(2,1)S(1)} collective-permute-done((bf16[16,4096]{1,0:T(8,128)(2,1)S(1)}, bf16[16,4096]{1,0:T(8,128)(2,1)S(1)}, u32[]{:S(2)}, u32[]{:S(2)}) %collective-permute-start.11) | collective-permute-done | bytes 131104 | tf_op jit(solution)/shard_map/ppermute | solution.py:50
  81.6 5.6 %collective-permute-done.12 = bf16[16,4096]{1,0:T(8,128)(2,1)S(1)} collective-permute-done((bf16[16,4096]{1,0:T(8,128)(2,1)S(1)}, bf16[16,4096]{1,0:T(8,128)(2,1)S(1)}, u32[]{:S(2)}, u32[]{:S(2)}) %collective-permute-start.12) | collective-permute-done | bytes 131104 | tf_op jit(solution)/shard_map/ppermute | solution.py:50
  88.3 14.8 %fusion = bf16[2,4096,1024]{2,1,0:T(8,128)(2,1)} fusion(bf16[2,4096,1024]{2,1,0:T(8,128)(2,1)} %param.9, f32[2,32,1024]{2,1,0:T(8,128)S(1)} %multiply_exponential_fusion), kind=kLoop, calls=%fused_computation.1 | loop fusion | flops 25165824 | bytes 33816576 | tf_op jit(solution)/shard_map/convert_element_type | solution.py:37
  127.1 32.3 %concatenate.6 = bf16[512,4096]{0,1:T(8,128)(2,1)} concatenate(bf16[16,4096]{0,1:T(8,128)(2,1)} %copy.10, bf16[16,4096]{0,1:T(8,128)(2,1)} %copy.11, bf16[16,4096]{0,1:T(8,128)(2,1)} %copy.12, bf16[16,4096]{0,1:T(8,128)(2,1)} %copy.13, bf16[16,4096]{0,1:T(8,128)(2,1)} %copy.14, bf16[16,4096]{0,1:T(8,128)(2,1)} %copy.15, bf16[16,4096]{0,1:T(8,128)(2,1)} %copy.16, ...), dimensions={0} | concatenate | bytes 8388608 | tf_op jit(solution)/shard_map/jit(_roll_dynamic)/concatenate | solution.py:51
  159.4 2.7 convert_multiply_fusion
  162.2 6.8 %fusion.11 = f32[256,64,64]{0,2,1:T(8,128)S(1)} fusion(f32[256,64,64]{0,2,1:T(8,128)S(1)} %bitcast.39), kind=kOutput, calls=%fused_computation.15 | convolution fusion | flops 805392384 | bytes 8388608 | tf_op jit(solution)/shard_map/ab,nbc,cd->nad/dot_general | solution.py:23
  169.0 6.1 %multiply_convert_fusion.1 = bf16[256,64,64]{0,2,1:T(8,128)(2,1)S(1)} fusion(f32[256,64,64]{0,2,1:T(8,128)S(1)} %fusion.11), kind=kOutput, calls=%fused_computation.17 | convolution fusion | flops 807489536 | bytes 6291456 | tf_op jit(solution)/shard_map/ab,nbc,cd->nad/dot_general | solution.py:23
  175.0 5.9 %fusion.2 = f32[256,1024]{1,0:T(8,128)S(1)} fusion(bf16[256,4096]{0,1:T(8,128)(2,1)S(1)} %bitcast.40, bf16[2,4096,1024]{2,1,0:T(8,128)(2,1)} %fusion), kind=kOutput, calls=%fused_computation.6 | convolution fusion | flops 2147483648 | bytes 11534336 | tf_op jit(solution)/shard_map/dot_general | solution.py:41
  181.0 2.4 fusion.19
  183.5 5.9 %fusion.3 = f32[256,1024]{1,0:T(8,128)S(1)} fusion(bf16[2,4096,1024]{2,1,0:T(8,128)(2,1)} %param.8, bf16[512,4096]{0,1:T(8,128)(2,1)S(1)} %copy-done, s32[]{:T(128)S(6)} %select_n.14), kind=kOutput, calls=%fused_computation.7 | convolution fusion | flops 2147483648 | bytes 11534340 | tf_op jit(solution)/shard_map/dot_general | solution.py:42
  189.3 13.5 %fusion.20 = f32[256,4096]{1,0:T(8,128)} fusion(bf16[1024,4096]{1,0:T(8,128)(2,1)} %param.11, bf16[256,1024]{1,0:T(8,128)(2,1)S(1)} %fusion.19, f32[256,1024]{1,0:T(8,128)S(1)} %fusion.3, bf16[2,4096,1024]{2,1,0:T(8,128)(2,1)} %param.8, bf16[512,4096]{0,1:T(8,128)(2,1)} %concatenate.6, s32[]{:T(128)S(6)} %select_n.14), kind=kOutput, calls=%fused_computation.26 | convolution fusion | flops 4297588736 | bytes 24641540 | tf_op jit(solution)/shard_map/dot_general | solution.py:58
  202.8 102.2 %all-reduce.1 = bf16[256,4096]{1,0:T(8,128)(2,1)S(1)} all-reduce(f32[256,4096]{1,0:T(8,128)} %fusion.20), channel_id=1, replica_groups=mesh['dom'=2,'tok'=16] {'tok'}, use_global_device_ids=true, to_apply=%region_0.1 | all-reduce | flops 1048576 | bytes 6291456 | tf_op jit(solution)/shard_map/psum | solution.py:59
  305.0 5.8 %multiply_convert_fusion = bf16[1024,4096]{1,0:T(8,128)(2,1)} fusion(bf16[256,1024]{1,0:T(8,128)(2,1)S(1)} %fusion.19, bf16[256,4096]{1,0:T(8,128)(2,1)S(1)} %all-reduce.1), kind=kOutput, calls=%fused_computation.2 | convolution fusion | flops 2155872256 | bytes 11010048 | tf_op jit(solution)/shard_map/dot_general | solution.py:60
  (76 shorter events, 33.1 us)
Async XLA Ops:
  0.0 4.9 %collective-permute-start = (bf16[16,4096]{1,0:T(8,128)(2,1)}, bf16[16,4096]{1,0:T(8,128)(2,1)S(1)}, u32[]{:S(2)}, u32[]{:S(2)}) collective-permute-start(bf16[16,4096]{1,0:T(8,128)(2,1)} %param.6), channel_id=1, source_target_pairs={{0,1},{1,2},{2,3},{3,4},{4,5},{5,6},{6,7},{7,8},{8,9},{9,10},{10,1... | collective-permute-start | bytes 393224 | tf_op jit(solution)/shard_map/ppermute | solution.py:50
  4.9 4.3 %collective-permute-start.1 = (bf16[16,4096]{1,0:T(8,128)(2,1)S(1)}, bf16[16,4096]{1,0:T(8,128)(2,1)S(1)}, u32[]{:S(2)}, u32[]{:S(2)}) collective-permute-start(bf16[16,4096]{1,0:T(8,128)(2,1)S(1)} %collective-permute-done), channel_id=1, source_target_pairs={{0,1},{1,2},{2,3},{3,4},{4,5},{5,6},{6,7},{7,8},{8,9},{9,10},{10,1... | collective-permute-start | bytes 393224 | tf_op jit(solution)/shard_map/ppermute | solution.py:50
  9.2 7.1 %collective-permute-start.2 = (bf16[16,4096]{1,0:T(8,128)(2,1)S(1)}, bf16[16,4096]{1,0:T(8,128)(2,1)S(1)}, u32[]{:S(2)}, u32[]{:S(2)}) collective-permute-start(bf16[16,4096]{1,0:T(8,128)(2,1)S(1)} %collective-permute-done.1), channel_id=1, source_target_pairs={{0,1},{1,2},{2,3},{3,4},{4,5},{5,6},{6,7},{7,8},{8,9},{9,10},{10,1... | collective-permute-start | bytes 393224 | tf_op jit(solution)/shard_map/ppermute | solution.py:50
  16.3 7.1 %collective-permute-start.3 = (bf16[16,4096]{1,0:T(8,128)(2,1)S(1)}, bf16[16,4096]{1,0:T(8,128)(2,1)S(1)}, u32[]{:S(2)}, u32[]{:S(2)}) collective-permute-start(bf16[16,4096]{1,0:T(8,128)(2,1)S(1)} %collective-permute-done.2), channel_id=1, source_target_pairs={{0,1},{1,2},{2,3},{3,4},{4,5},{5,6},{6,7},{7,8},{8,9},{9,10},{10,1... | collective-permute-start | bytes 393224 | tf_op jit(solution)/shard_map/ppermute | solution.py:50
  23.4 7.1 %collective-permute-start.4 = (bf16[16,4096]{1,0:T(8,128)(2,1)S(1)}, bf16[16,4096]{1,0:T(8,128)(2,1)S(1)}, u32[]{:S(2)}, u32[]{:S(2)}) collective-permute-start(bf16[16,4096]{1,0:T(8,128)(2,1)S(1)} %collective-permute-done.3), channel_id=1, source_target_pairs={{0,1},{1,2},{2,3},{3,4},{4,5},{5,6},{6,7},{7,8},{8,9},{9,10},{10,1... | collective-permute-start | bytes 393224 | tf_op jit(solution)/shard_map/ppermute | solution.py:50
  30.5 72.6 %copy-start.1 = (bf16[16,4096]{1,0:T(8,128)(2,1)}, bf16[16,4096]{1,0:T(8,128)(2,1)S(1)}, u32[]{:S(2)}) copy-start(bf16[16,4096]{1,0:T(8,128)(2,1)S(1)} %collective-permute-done.4) | copy-start | bytes 393220
  30.5 7.1 %collective-permute-start.5 = (bf16[16,4096]{1,0:T(8,128)(2,1)S(1)}, bf16[16,4096]{1,0:T(8,128)(2,1)S(1)}, u32[]{:S(2)}, u32[]{:S(2)}) collective-permute-start(bf16[16,4096]{1,0:T(8,128)(2,1)S(1)} %collective-permute-done.4), channel_id=1, source_target_pairs={{0,1},{1,2},{2,3},{3,4},{4,5},{5,6},{6,7},{7,8},{8,9},{9,10},{10,1... | collective-permute-start | bytes 393224 | tf_op jit(solution)/shard_map/ppermute | solution.py:50
  37.6 65.5 %copy-start.2 = (bf16[16,4096]{1,0:T(8,128)(2,1)}, bf16[16,4096]{1,0:T(8,128)(2,1)S(1)}, u32[]{:S(2)}) copy-start(bf16[16,4096]{1,0:T(8,128)(2,1)S(1)} %collective-permute-done.5) | copy-start | bytes 393220
  37.6 7.1 %collective-permute-start.6 = (bf16[16,4096]{1,0:T(8,128)(2,1)S(1)}, bf16[16,4096]{1,0:T(8,128)(2,1)S(1)}, u32[]{:S(2)}, u32[]{:S(2)}) collective-permute-start(bf16[16,4096]{1,0:T(8,128)(2,1)S(1)} %collective-permute-done.5), channel_id=1, source_target_pairs={{0,1},{1,2},{2,3},{3,4},{4,5},{5,6},{6,7},{7,8},{8,9},{9,10},{10,1... | collective-permute-start | bytes 393224 | tf_op jit(solution)/shard_map/ppermute | solution.py:50
  44.7 58.4 %copy-start.3 = (bf16[16,4096]{1,0:T(8,128)(2,1)}, bf16[16,4096]{1,0:T(8,128)(2,1)S(1)}, u32[]{:S(2)}) copy-start(bf16[16,4096]{1,0:T(8,128)(2,1)S(1)} %collective-permute-done.6) | copy-start | bytes 393220
  44.7 7.1 %collective-permute-start.7 = (bf16[16,4096]{1,0:T(8,128)(2,1)S(1)}, bf16[16,4096]{1,0:T(8,128)(2,1)S(1)}, u32[]{:S(2)}, u32[]{:S(2)}) collective-permute-start(bf16[16,4096]{1,0:T(8,128)(2,1)S(1)} %collective-permute-done.6), channel_id=1, source_target_pairs={{0,1},{1,2},{2,3},{3,4},{4,5},{5,6},{6,7},{7,8},{8,9},{9,10},{10,1... | collective-permute-start | bytes 393224 | tf_op jit(solution)/shard_map/ppermute | solution.py:50
  51.7 51.3 %copy-start.5 = (bf16[16,4096]{1,0:T(8,128)(2,1)}, bf16[16,4096]{1,0:T(8,128)(2,1)S(1)}, u32[]{:S(2)}) copy-start(bf16[16,4096]{1,0:T(8,128)(2,1)S(1)} %collective-permute-done.7) | copy-start | bytes 393220
  51.7 7.1 %collective-permute-start.8 = (bf16[16,4096]{1,0:T(8,128)(2,1)S(1)}, bf16[16,4096]{1,0:T(8,128)(2,1)S(1)}, u32[]{:S(2)}, u32[]{:S(2)}) collective-permute-start(bf16[16,4096]{1,0:T(8,128)(2,1)S(1)} %collective-permute-done.7), channel_id=1, source_target_pairs={{0,1},{1,2},{2,3},{3,4},{4,5},{5,6},{6,7},{7,8},{8,9},{9,10},{10,1... | collective-permute-start | bytes 393224 | tf_op jit(solution)/shard_map/ppermute | solution.py:50
  58.8 44.2 %copy-start.7 = (bf16[16,4096]{1,0:T(8,128)(2,1)}, bf16[16,4096]{1,0:T(8,128)(2,1)S(1)}, u32[]{:S(2)}) copy-start(bf16[16,4096]{1,0:T(8,128)(2,1)S(1)} %collective-permute-done.8) | copy-start | bytes 393220
  58.8 7.1 %collective-permute-start.9 = (bf16[16,4096]{1,0:T(8,128)(2,1)S(1)}, bf16[16,4096]{1,0:T(8,128)(2,1)S(1)}, u32[]{:S(2)}, u32[]{:S(2)}) collective-permute-start(bf16[16,4096]{1,0:T(8,128)(2,1)S(1)} %collective-permute-done.8), channel_id=1, source_target_pairs={{0,1},{1,2},{2,3},{3,4},{4,5},{5,6},{6,7},{7,8},{8,9},{9,10},{10,1... | collective-permute-start | bytes 393224 | tf_op jit(solution)/shard_map/ppermute | solution.py:50
  65.9 37.1 %copy-start.9 = (bf16[16,4096]{1,0:T(8,128)(2,1)}, bf16[16,4096]{1,0:T(8,128)(2,1)S(1)}, u32[]{:S(2)}) copy-start(bf16[16,4096]{1,0:T(8,128)(2,1)S(1)} %collective-permute-done.9) | copy-start | bytes 393220
  65.9 7.1 %collective-permute-start.10 = (bf16[16,4096]{1,0:T(8,128)(2,1)S(1)}, bf16[16,4096]{1,0:T(8,128)(2,1)S(1)}, u32[]{:S(2)}, u32[]{:S(2)}) collective-permute-start(bf16[16,4096]{1,0:T(8,128)(2,1)S(1)} %collective-permute-done.9), channel_id=1, source_target_pairs={{0,1},{1,2},{2,3},{3,4},{4,5},{5,6},{6,7},{7,8},{8,9},{9,10},{10,1... | collective-permute-start | bytes 393224 | tf_op jit(solution)/shard_map/ppermute | solution.py:50
  73.0 30.0 %copy-start.10 = (bf16[16,4096]{1,0:T(8,128)(2,1)}, bf16[16,4096]{1,0:T(8,128)(2,1)S(1)}, u32[]{:S(2)}) copy-start(bf16[16,4096]{1,0:T(8,128)(2,1)S(1)} %collective-permute-done.10) | copy-start | bytes 393220
  73.0 7.1 %collective-permute-start.11 = (bf16[16,4096]{1,0:T(8,128)(2,1)S(1)}, bf16[16,4096]{1,0:T(8,128)(2,1)S(1)}, u32[]{:S(2)}, u32[]{:S(2)}) collective-permute-start(bf16[16,4096]{1,0:T(8,128)(2,1)S(1)} %collective-permute-done.10), channel_id=1, source_target_pairs={{0,1},{1,2},{2,3},{3,4},{4,5},{5,6},{6,7},{7,8},{8,9},{9,10},{10,1... | collective-permute-start | bytes 393224 | tf_op jit(solution)/shard_map/ppermute | solution.py:50
  80.1 23.0 %copy-start.11 = (bf16[16,4096]{1,0:T(8,128)(2,1)}, bf16[16,4096]{1,0:T(8,128)(2,1)S(1)}, u32[]{:S(2)}) copy-start(bf16[16,4096]{1,0:T(8,128)(2,1)S(1)} %collective-permute-done.11) | copy-start | bytes 393220
  80.1 7.1 %collective-permute-start.12 = (bf16[16,4096]{1,0:T(8,128)(2,1)S(1)}, bf16[16,4096]{1,0:T(8,128)(2,1)S(1)}, u32[]{:S(2)}, u32[]{:S(2)}) collective-permute-start(bf16[16,4096]{1,0:T(8,128)(2,1)S(1)} %collective-permute-done.11), channel_id=1, source_target_pairs={{0,1},{1,2},{2,3},{3,4},{4,5},{5,6},{6,7},{7,8},{8,9},{9,10},{10,1... | collective-permute-start | bytes 393224 | tf_op jit(solution)/shard_map/ppermute | solution.py:50
  87.2 15.9 %collective-permute-start.13 = (bf16[16,4096]{1,0:T(8,128)(2,1)S(1)}, bf16[16,4096]{1,0:T(8,128)(2,1)}, u32[]{:S(2)}, u32[]{:S(2)}) collective-permute-start(bf16[16,4096]{1,0:T(8,128)(2,1)S(1)} %collective-permute-done.12), channel_id=1, source_target_pairs={{0,1},{1,2},{2,3},{3,4},{4,5},{5,6},{6,7},{7,8},{8,9},{9,10},{10,1... | collective-permute-start | bytes 393224 | tf_op jit(solution)/shard_map/ppermute | solution.py:50
  103.1 21.8 %collective-permute-start.14 = (bf16[16,4096]{1,0:T(8,128)(2,1)}, bf16[16,4096]{1,0:T(8,128)(2,1)}, u32[]{:S(2)}, u32[]{:S(2)}) collective-permute-start(bf16[16,4096]{1,0:T(8,128)(2,1)} %collective-permute-done.13), channel_id=1, source_target_pairs={{0,1},{1,2},{2,3},{3,4},{4,5},{5,6},{6,7},{7,8},{8,9},{9,10},{10,1... | collective-permute-start | bytes 393224 | tf_op jit(solution)/shard_map/ppermute | solution.py:50
  162.2 18.8 %slice-start = ((s8[16777216]{0:T(1024)(128)(4,1)}), s8[4194304]{0:T(1024)(128)(4,1)S(1)}, s32[]{:S(2)}) async-start(s8[16777216]{0:T(1024)(128)(4,1)} %bitcast.37), calls=%async_computation | async-start | bytes 8388608
  (11 other events, 100.0 us)
